TPU v7x, 32 devices: a whole 2x2x4 slice. The times are simulated.
32 devices in a mesh: groups: 2 (over y), slices: 8 (over z, x), ering: 2 (over core).
Axes of the slice: x: 2, y: 2, z: 4, core: 2. Of those that a mesh axis runs over, the one named last changes fastest.
Arguments:
- positions: float32 [3, 128, 256], P(None, ('groups', 'slices'), 'ering'), parts along dimension 1, may hold values from -9 to 9
- hidden: bfloat16 [128, 256, 256], P(('groups', 'slices'), 'ering'), parts along dimension 0, may hold values from -6 to 6
- cotangent: bfloat16 [128, 256, 256], P(('groups', 'slices'), 'ering'), parts along dimension 0, may hold values from -6 to 6
- embed_weight: float32 [32, 4], replicated, may hold values from -3 to 3
- embed_bias: float32 [32], replicated, may hold values from -3 to 3
- pair_weight: bfloat16 [32, 32], replicated, may hold values from -1 to 1
- pair_bias: float32 [32], replicated, may hold values from -3 to 3
- one_weight: bfloat16 [256, 256], replicated, may hold values from -0.375 to 0.375
- pool_weight: bfloat16 [32, 256], replicated, may hold values from -1 to 1
- mean_weight: bfloat16 [256, 256], replicated, may hold values from -0.375 to 0.375
- one_bias: float32 [256], replicated, may hold values from -3 to 3
- drift_weight: bfloat16 [3, 256], replicated, may hold values from -0.375 to 0.375
Outputs:
- updated: bfloat16 [128, 256, 256], P(('groups', 'slices'), 'ering'), parts along dimension 0
- hidden_grad: bfloat16 [128, 256, 256], P(('groups', 'slices'), 'ering'), parts along dimension 0
- link_terms: float32 [128, 256], P(('groups', 'slices'), 'ering'), parts along dimension 0
- pair_grad: float32 [64, 32], P('groups'), parts along dimension 0
- bias_grad: float32 [64], P('groups'), parts along dimension 0
- one_grad: float32 [512, 256], P('groups'), parts along dimension 0
- pool_grad: float32 [64, 256], P('groups'), parts along dimension 0
- mean_grad: float32 [512, 256], P('groups'), parts along dimension 0
There are 2 independent parts, one for each index of `groups`. A program takes and returns all parts, laid end to end along the dimension named above; an argument that names none is the same for every part. Nothing has to cross between parts.
All inputs are finite; a program needn't handle non-finite values.
Results may differ from a plain program's by a relative error of at most 0.0054.
Values may be sent and summed in bfloat16 or wider, within the bound.
No kernel may reach another device: no remote copies, remote signals or barrier semaphores. Data moves between devices by JAX's collectives and lax.ppermute only.
A program may use at most 64 MiB of HBM per device.

v0:
```python
import math
import jax
import jax.numpy as jnp
from jax import lax
from jax.sharding import PartitionSpec as P

HIGH = lax.Precision.HIGHEST
step_tau = 0.5


def from_behind(array, axis, by):
    size = lax.axis_size(axis)
    pairs = [(i, i + by) for i in range(size) if 0 <= i + by < size]
    return lax.ppermute(array, axis, pairs)


def local(
    positions,
    hidden,
    cotangent,
    embed_weight,
    embed_bias,
    pair_weight,
    pair_bias,
    one_weight,
    pool_weight,
    mean_weight,
    one_bias,
    drift_weight,
):
    own_count = hidden.shape[1]
    total_count = own_count * lax.axis_size("ering")
    slab_count = hidden.shape[0]
    scale = 1.0 / math.sqrt(slab_count * lax.axis_size("slices") * total_count)
    every_pos = lax.all_gather(positions, "ering", axis=2, tiled=True)
    full_rows = lax.all_gather(hidden, "ering", axis=1, tiled=True)
    mean_rows = (jnp.sum(full_rows.astype(jnp.float32), axis=1) / total_count).astype(jnp.bfloat16)

    def one_slice(carry, inputs):
        own_pos, all_pos, hid_s, cot_s, mean_s = inputs
        offsets = own_pos[:, :, None] - all_pos[:, None, :]
        radial = jnp.sqrt(jnp.sum(offsets * offsets, axis=0) + 1.0)
        features = jnp.concatenate([offsets, radial[None]], axis=0)
        pair_in = jnp.tanh(
            jnp.einsum("ck,kij->cij", embed_weight, features, precision=HIGH)
            + embed_bias[:, None, None]
        ).astype(jnp.bfloat16)
        pair_pre = (
            jnp.einsum("ck,kij->cij", pair_weight, pair_in, preferred_element_type=jnp.float32)
            + pair_bias[:, None, None]
        )
        pair_act = jnp.tanh(pair_pre)
        pooled = jnp.mean(pair_act + pair_in.astype(jnp.float32), axis=2).T.astype(jnp.bfloat16)
        one_pre = jnp.dot(hid_s, one_weight, preferred_element_type=jnp.float32)
        one_pre = one_pre + jnp.dot(pooled, pool_weight, preferred_element_type=jnp.float32)
        one_pre = (
            one_pre
            + jnp.dot(mean_s[None, :], mean_weight, preferred_element_type=jnp.float32)
            + one_bias
        )
        one_act = jnp.tanh(one_pre)
        updated = (one_act + hid_s.astype(jnp.float32)).astype(jnp.bfloat16)
        pre_grad = (cot_s.astype(jnp.float32) * (1.0 - one_act * one_act)).astype(jnp.bfloat16)
        column_part = jnp.sum(pre_grad.astype(jnp.float32), axis=0)
        pooled_grad = jnp.dot(pre_grad, pool_weight.T, preferred_element_type=jnp.float32)
        partial_grad = cot_s.astype(jnp.float32) + jnp.dot(
            pre_grad, one_weight.T, preferred_element_type=jnp.float32
        )
        act_grad = pooled_grad.T[:, :, None] / total_count * (1.0 - pair_act * pair_act)
        act_low = act_grad.astype(jnp.bfloat16)
        weight_term = jnp.einsum(
            "cij,kij->ck", act_low, pair_in, preferred_element_type=jnp.float32
        )
        bias_term = jnp.sum(act_grad, axis=(1, 2))
        carry = (
            carry[0] + weight_term,
            carry[1] + bias_term,
            carry[2] + jnp.einsum("id,ie->de", hid_s, pre_grad, preferred_element_type=jnp.float32),
            carry[3]
            + jnp.einsum("ic,ie->ce", pooled, pre_grad, preferred_element_type=jnp.float32),
        )
        return (carry, (updated, partial_grad, column_part))

    d_one = hidden.shape[2]
    p_width = pair_weight.shape[0]
    start = (
        jnp.zeros((p_width, p_width), jnp.float32),
        jnp.zeros((p_width,), jnp.float32),
        jnp.zeros((d_one, d_one), jnp.float32),
        jnp.zeros((p_width, d_one), jnp.float32),
    )
    inputs = (
        jnp.moveaxis(positions, 1, 0),
        jnp.moveaxis(every_pos, 1, 0),
        hidden,
        cotangent,
        mean_rows,
    )
    totals, (updated, partial_grad, column_parts) = lax.scan(one_slice, start, inputs)
    column_total = lax.psum(column_parts, "ering")
    mean_back = jnp.dot(column_total, mean_weight.astype(jnp.float32).T, precision=HIGH)
    hidden_grad = (partial_grad + mean_back[:, None, :] / total_count).astype(jnp.bfloat16)
    mean_term = jnp.dot(mean_rows.astype(jnp.float32).T, column_parts, precision=HIGH)
    grads = (totals[0], totals[1], totals[2], totals[3], mean_term)
    grads = lax.psum((grads[0], grads[1], grads[2], grads[3], grads[4]), ("slices", "ering"))
    drift = jnp.einsum(
        "cd,sid->csi", drift_weight.astype(jnp.float32), updated.astype(jnp.float32), precision=HIGH
    )
    first_next = from_behind(positions[:, :1, :], "slices", -1)
    following = jnp.concatenate([positions[:, 1:], first_next], axis=1)
    jump = following - positions - step_tau * drift
    link_terms = jnp.sum(jump * jump, axis=0) / (12.0 * step_tau)
    is_last = lax.axis_index("slices") == lax.axis_size("slices") - 1
    last_row = jnp.logical_and(is_last, jnp.arange(slab_count) == slab_count - 1)
    link_terms = jnp.where(last_row[:, None], jnp.float32(0.0), link_terms)
    return (
        updated,
        hidden_grad,
        link_terms,
        scale * grads[0],
        scale * grads[1],
        scale * grads[2],
        scale * grads[3],
        scale * grads[4],
    )


def solution(mesh):
    in_specs = (
        P(None, ("groups", "slices"), "ering"),
        P(("groups", "slices"), "ering", None),
        P(("groups", "slices"), "ering", None),
        P(),
        P(),
        P(),
        P(),
        P(),
        P(),
        P(),
        P(),
        P(),
    )
    out_specs = (
        P(("groups", "slices"), "ering", None),
        P(("groups", "slices"), "ering", None),
        P(("groups", "slices"), "ering"),
        P("groups", None),
        P("groups"),
        P("groups", None),
        P("groups", None),
        P("groups", None),
    )
    return jax.shard_map(local, mesh=mesh, in_specs=in_specs, out_specs=out_specs, check_vma=False)
```

profile of v0, /device:TPU:1, one launch (start us, length us, event | category | flops | bytes accessed | tf_op | source)
XLA Modules:
  0.0 349.7 jit_solution(2469969843966175401)
XLA Ops:
  12.8 8.3 %all-gather.2.cloned.1.call-done = bf16[8,256,256]{2,1,0:T(8,128)(2,1)} async-done(((bf16[8,128,256]{2,1,0:T(8,128)(2,1)}), bf16[8,256,256]{2,1,0:T(8,128)(2,1)}) %all-gather.2.cloned.1.call-update) | async-done | bytes 1048592 | tf_op jit(solution)/shard_map/all_gather | solution.py:36
  22.5 160.3 %while.23 = (s32[]{:T(128)}, f32[32,32]{1,0:T(8,128)S(1)}, f32[32]{0:T(128)S(1)}, f32[256,256]{1,0:T(8,128)S(1)}, f32[32,256]{1,0:T(8,128)S(1)}, /*index=5*/bf16...) while((s32[]{:T(128)}, f32[32,32]{1,0:T(8,128)S(1)}, ...), condition=%wide.region_6.7_spmd.clone, body=%wide.region_1.6_spmd.clone.sunk | while | flops 259163936 | bytes 40384416 | solution.py:99
  24.3 4.5 %tanh_convert_fusion.2 = bf16[128,256,32]{1,2,0:T(8,128)(2,1)S(1)} fusion(f32[32]{0:T(128)} %get-tuple-element.451, f32[1,128,256]{2,0,1:T(1,128)S(1)} %copy.37, f32[3,128,256]{2,0,1:T(4,128)S(1)} %get-tuple-element.385, f32[32,4]{0,1:T(4,128)} %get-tuple-element.450), kind=kOutput, calls=%fused_computation.6.clone.1 | convolution fusion | flops 52559872 | bytes 2622080 | tf_op jit(solution)/shard_map/while/body/eval_jaxpr/ck,kij->cij/dot_general | solution.py:45
  28.8 2.7 fusion.111
  33.3 3.5 fusion.115
  44.3 4.5 %tanh_convert_fusion.2 = bf16[128,256,32]{1,2,0:T(8,128)(2,1)S(1)} fusion(f32[32]{0:T(128)} %get-tuple-element.451, f32[1,128,256]{2,0,1:T(1,128)S(1)} %copy.37, f32[3,128,256]{2,0,1:T(4,128)S(1)} %get-tuple-element.385, f32[32,4]{0,1:T(4,128)} %get-tuple-element.450), kind=kOutput, calls=%fused_computation.6.clone.1 | convolution fusion | flops 52559872 | bytes 2622080 | tf_op jit(solution)/shard_map/while/body/eval_jaxpr/ck,kij->cij/dot_general | solution.py:45
  48.8 2.7 fusion.111
  53.3 3.5 fusion.115
  64.3 4.5 %tanh_convert_fusion.2 = bf16[128,256,32]{1,2,0:T(8,128)(2,1)S(1)} fusion(f32[32]{0:T(128)} %get-tuple-element.451, f32[1,128,256]{2,0,1:T(1,128)S(1)} %copy.37, f32[3,128,256]{2,0,1:T(4,128)S(1)} %get-tuple-element.385, f32[32,4]{0,1:T(4,128)} %get-tuple-element.450), kind=kOutput, calls=%fused_computation.6.clone.1 | convolution fusion | flops 52559872 | bytes 2622080 | tf_op jit(solution)/shard_map/while/body/eval_jaxpr/ck,kij->cij/dot_general | solution.py:45
  68.9 2.7 fusion.111
  73.3 3.5 fusion.115
  84.4 4.5 %tanh_convert_fusion.2 = bf16[128,256,32]{1,2,0:T(8,128)(2,1)S(1)} fusion(f32[32]{0:T(128)} %get-tuple-element.451, f32[1,128,256]{2,0,1:T(1,128)S(1)} %copy.37, f32[3,128,256]{2,0,1:T(4,128)S(1)} %get-tuple-element.385, f32[32,4]{0,1:T(4,128)} %get-tuple-element.450), kind=kOutput, calls=%fused_computation.6.clone.1 | convolution fusion | flops 52559872 | bytes 2622080 | tf_op jit(solution)/shard_map/while/body/eval_jaxpr/ck,kij->cij/dot_general | solution.py:45
  93.4 3.5 fusion.115
  104.4 4.5 %tanh_convert_fusion.2 = bf16[128,256,32]{1,2,0:T(8,128)(2,1)S(1)} fusion(f32[32]{0:T(128)} %get-tuple-element.451, f32[1,128,256]{2,0,1:T(1,128)S(1)} %copy.37, f32[3,128,256]{2,0,1:T(4,128)S(1)} %get-tuple-element.385, f32[32,4]{0,1:T(4,128)} %get-tuple-element.450), kind=kOutput, calls=%fused_computation.6.clone.1 | convolution fusion | flops 52559872 | bytes 2622080 | tf_op jit(solution)/shard_map/while/body/eval_jaxpr/ck,kij->cij/dot_general | solution.py:45
  113.4 3.5 fusion.115
  124.4 4.5 %tanh_convert_fusion.2 = bf16[128,256,32]{1,2,0:T(8,128)(2,1)S(1)} fusion(f32[32]{0:T(128)} %get-tuple-element.451, f32[1,128,256]{2,0,1:T(1,128)S(1)} %copy.37, f32[3,128,256]{2,0,1:T(4,128)S(1)} %get-tuple-element.385, f32[32,4]{0,1:T(4,128)} %get-tuple-element.450), kind=kOutput, calls=%fused_computation.6.clone.1 | convolution fusion | flops 52559872 | bytes 2622080 | tf_op jit(solution)/shard_map/while/body/eval_jaxpr/ck,kij->cij/dot_general | solution.py:45
  129.0 2.7 fusion.111
  133.4 3.5 fusion.115
  144.5 4.5 %tanh_convert_fusion.2 = bf16[128,256,32]{1,2,0:T(8,128)(2,1)S(1)} fusion(f32[32]{0:T(128)} %get-tuple-element.451, f32[1,128,256]{2,0,1:T(1,128)S(1)} %copy.37, f32[3,128,256]{2,0,1:T(4,128)S(1)} %get-tuple-element.385, f32[32,4]{0,1:T(4,128)} %get-tuple-element.450), kind=kOutput, calls=%fused_computation.6.clone.1 | convolution fusion | flops 52559872 | bytes 2622080 | tf_op jit(solution)/shard_map/while/body/eval_jaxpr/ck,kij->cij/dot_general | solution.py:45
  153.5 3.5 fusion.115
  164.5 4.5 %tanh_convert_fusion.2 = bf16[128,256,32]{1,2,0:T(8,128)(2,1)S(1)} fusion(f32[32]{0:T(128)} %get-tuple-element.451, f32[1,128,256]{2,0,1:T(1,128)S(1)} %copy.37, f32[3,128,256]{2,0,1:T(4,128)S(1)} %get-tuple-element.385, f32[32,4]{0,1:T(4,128)} %get-tuple-element.450), kind=kOutput, calls=%fused_computation.6.clone.1 | convolution fusion | flops 52559872 | bytes 2622080 | tf_op jit(solution)/shard_map/while/body/eval_jaxpr/ck,kij->cij/dot_general | solution.py:45
  173.5 3.5 fusion.115
  186.3 57.3 %all-reduce = (f32[32,32]{1,0:T(8,128)S(1)}, f32[32]{0:T(128)S(1)}, f32[32,256]{1,0:T(8,128)S(1)}) all-reduce(f32[32,32]{1,0:T(8,128)S(1)} %get-tuple-element.124, f32[32]{0:T(128)S(1)} %get-tuple-element.125, f32[32,256]{1,0:T(8,128)S(1)} %get-tuple-element.127), channel_id=1, replica_groups=mesh['groups'=2,'slices'=8,'ering'=2] {'slices','ering'}, use_global_device_ids=true, to_apply=%region_9.10 | all-reduce | flops 9248 | bytes 73984 | tf_op jit(solution)/shard_map/psum | solution.py:105
  250.6 90.4 %all-reduce.4.cloned.1.call-done = (f32[256,256]{1,0:T(8,128)}, f32[256,256]{1,0:T(8,128)}) async-done(((f32[256,256]{1,0:T(8,128)}, f32[256,256]{1,0:T(8,128)}), (f32[256,256]{1,0:T(8,128)}, f32[256,256]{1,0:T(8,128)})) %all-reduce.4.cloned.1.call-update) | async-done | bytes 524304 | tf_op jit(solution)/shard_map/psum | solution.py:105
  (273 shorter events, 103.2 us)
Async XLA Ops:
  7.2 239.3 %copy-start = (bf16[3,256]{1,0:T(4,128)(2,1)S(1)}, bf16[3,256]{1,0:T(4,128)(2,1)}, u32[]{:S(2)}) copy-start(bf16[3,256]{1,0:T(4,128)(2,1)} %param.25) | copy-start | bytes 4612
  7.2 13.9 %all-gather.2.cloned.1.call-start = ((), (), s32[]{:S(2)}) async-start(), calls=%async_computation | async-start | bytes 1572864 | tf_op jit(solution)/shard_map/all_gather | solution.py:36
  7.9 333.1 %all-reduce.4.cloned.1.call-start = ((), (), s32[]{:S(2)}) async-start(), calls=%async_computation.1 | async-start | bytes 1048576 | tf_op jit(solution)/shard_map/psum | solution.py:105
  8.7 237.8 %collective-permute-start = (f32[3,1,128]{2,0,1:T(4,128)S(1)}, f32[3,1,128]{2,0,1:T(4,128)S(1)}, u32[]{:S(2)}, u32[]{:S(2)}) collective-permute-start(f32[3,1,128]{2,0,1:T(4,128)S(1)} %slice.9), channel_id=1, source_target_pairs={{2,0},{4,2},{6,4},{8,6},{10,8},{12,10},{14,12},{3,1},{5,3},{7,5},{... | collective-permute-start | bytes 4616 | tf_op jit(solution)/shard_map/ppermute | solution.py:14
  22.5 224.0 %copy-start.6 = (f32[3,8,128]{2,1,0:T(8,128)S(1)}, f32[3,8,128]{2,1,0:T(8,128)}, u32[]{:S(2)}) copy-start(f32[3,8,128]{2,1,0:T(8,128)} %param.14) | copy-start | bytes 36868
  24.2 7.5 %copy-start.2 = (bf16[256,256]{1,0:T(8,128)(2,1)S(1)}, bf16[256,256]{1,0:T(8,128)(2,1)}, u32[]{:S(2)}) copy-start(bf16[256,256]{1,0:T(8,128)(2,1)} %get-tuple-element.447) | copy-start | bytes 393220 | tf_op jit(solution)/shard_map/while
  24.2 7.5 %copy-start.8 = (f32[256]{0:T(256)S(1)}, f32[256]{0:T(256)}, u32[]{:S(2)}) copy-start(f32[256]{0:T(256)} %get-tuple-element.457) | copy-start | bytes 3076 | tf_op jit(solution)/shard_map/while
  44.3 7.5 %copy-start.2 = (bf16[256,256]{1,0:T(8,128)(2,1)S(1)}, bf16[256,256]{1,0:T(8,128)(2,1)}, u32[]{:S(2)}) copy-start(bf16[256,256]{1,0:T(8,128)(2,1)} %get-tuple-element.447) | copy-start | bytes 393220 | tf_op jit(solution)/shard_map/while
  44.3 7.5 %copy-start.8 = (f32[256]{0:T(256)S(1)}, f32[256]{0:T(256)}, u32[]{:S(2)}) copy-start(f32[256]{0:T(256)} %get-tuple-element.457) | copy-start | bytes 3076 | tf_op jit(solution)/shard_map/while
  64.3 7.5 %copy-start.2 = (bf16[256,256]{1,0:T(8,128)(2,1)S(1)}, bf16[256,256]{1,0:T(8,128)(2,1)}, u32[]{:S(2)}) copy-start(bf16[256,256]{1,0:T(8,128)(2,1)} %get-tuple-element.447) | copy-start | bytes 393220 | tf_op jit(solution)/shard_map/while
  64.3 7.5 %copy-start.8 = (f32[256]{0:T(256)S(1)}, f32[256]{0:T(256)}, u32[]{:S(2)}) copy-start(f32[256]{0:T(256)} %get-tuple-element.457) | copy-start | bytes 3076 | tf_op jit(solution)/shard_map/while
  84.3 7.3 %copy-start.4 = (bf16[32,256]{1,0:T(8,128)(2,1)S(1)}, bf16[32,256]{1,0:T(8,128)(2,1)}, u32[]{:S(2)}) copy-start(bf16[32,256]{1,0:T(8,128)(2,1)} %get-tuple-element.454) | copy-start | bytes 49156 | tf_op jit(solution)/shard_map/while
  84.3 7.5 %copy-start.2 = (bf16[256,256]{1,0:T(8,128)(2,1)S(1)}, bf16[256,256]{1,0:T(8,128)(2,1)}, u32[]{:S(2)}) copy-start(bf16[256,256]{1,0:T(8,128)(2,1)} %get-tuple-element.447) | copy-start | bytes 393220 | tf_op jit(solution)/shard_map/while
  84.3 7.5 %copy-start.8 = (f32[256]{0:T(256)S(1)}, f32[256]{0:T(256)}, u32[]{:S(2)}) copy-start(f32[256]{0:T(256)} %get-tuple-element.457) | copy-start | bytes 3076 | tf_op jit(solution)/shard_map/while
  104.4 7.3 %copy-start.4 = (bf16[32,256]{1,0:T(8,128)(2,1)S(1)}, bf16[32,256]{1,0:T(8,128)(2,1)}, u32[]{:S(2)}) copy-start(bf16[32,256]{1,0:T(8,128)(2,1)} %get-tuple-element.454) | copy-start | bytes 49156 | tf_op jit(solution)/shard_map/while
  104.4 7.5 %copy-start.2 = (bf16[256,256]{1,0:T(8,128)(2,1)S(1)}, bf16[256,256]{1,0:T(8,128)(2,1)}, u32[]{:S(2)}) copy-start(bf16[256,256]{1,0:T(8,128)(2,1)} %get-tuple-element.447) | copy-start | bytes 393220 | tf_op jit(solution)/shard_map/while
  104.4 7.5 %copy-start.8 = (f32[256]{0:T(256)S(1)}, f32[256]{0:T(256)}, u32[]{:S(2)}) copy-start(f32[256]{0:T(256)} %get-tuple-element.457) | copy-start | bytes 3076 | tf_op jit(solution)/shard_map/while
  124.4 7.5 %copy-start.2 = (bf16[256,256]{1,0:T(8,128)(2,1)S(1)}, bf16[256,256]{1,0:T(8,128)(2,1)}, u32[]{:S(2)}) copy-start(bf16[256,256]{1,0:T(8,128)(2,1)} %get-tuple-element.447) | copy-start | bytes 393220 | tf_op jit(solution)/shard_map/while
  124.4 7.5 %copy-start.8 = (f32[256]{0:T(256)S(1)}, f32[256]{0:T(256)}, u32[]{:S(2)}) copy-start(f32[256]{0:T(256)} %get-tuple-element.457) | copy-start | bytes 3076 | tf_op jit(solution)/shard_map/while
  144.5 7.5 %copy-start.2 = (bf16[256,256]{1,0:T(8,128)(2,1)S(1)}, bf16[256,256]{1,0:T(8,128)(2,1)}, u32[]{:S(2)}) copy-start(bf16[256,256]{1,0:T(8,128)(2,1)} %get-tuple-element.447) | copy-start | bytes 393220 | tf_op jit(solution)/shard_map/while
  144.5 7.5 %copy-start.8 = (f32[256]{0:T(256)S(1)}, f32[256]{0:T(256)}, u32[]{:S(2)}) copy-start(f32[256]{0:T(256)} %get-tuple-element.457) | copy-start | bytes 3076 | tf_op jit(solution)/shard_map/while
  164.5 7.5 %copy-start.2 = (bf16[256,256]{1,0:T(8,128)(2,1)S(1)}, bf16[256,256]{1,0:T(8,128)(2,1)}, u32[]{:S(2)}) copy-start(bf16[256,256]{1,0:T(8,128)(2,1)} %get-tuple-element.447) | copy-start | bytes 393220 | tf_op jit(solution)/shard_map/while
  164.5 7.5 %copy-start.8 = (f32[256]{0:T(256)S(1)}, f32[256]{0:T(256)}, u32[]{:S(2)}) copy-start(f32[256]{0:T(256)} %get-tuple-element.457) | copy-start | bytes 3076 | tf_op jit(solution)/shard_map/while
  182.8 65.7 %copy-start.3 = (f32[256,256]{1,0:T(8,128)}, f32[256,256]{1,0:T(8,128)S(1)}, u32[]{:S(2)}) copy-start(f32[256,256]{1,0:T(8,128)S(1)} %get-tuple-element.126) | copy-start | bytes 786436
  (30 other events, 172.8 us)
Sparse Core Ops, SparseCore 0:
  9.6 11.4 all-gather.1
  248.6 92.3 all-reduce.3
where the time goes:
time: 352 us; the launch traced here: 350 us
  matrix products  132 us (38%)
  waiting for transfers between devices  99.3 us (28%)
  blocking collectives  61.6 us (18%)
  other arithmetic  35.4 us (10%)
  between operations  14.2 us (4%)
  local copies, waits for them, and re-layouts  4.24 us (1%)
    psum x1, waiting for transfers between devices, local(): lax.psum((grads[0], grads[1], grads[2], grads[3], grads[4]), ('slices', '...  90.4 us
    psum x1, blocking collectives, local(): lax.psum((grads[0], grads[1], grads[2], grads[3], grads[4]), ('slices', '...  57.3 us
    dot_general x8, matrix products, one_slice(): jnp.einsum('ck,kij->cij', embed_weight, features, precision=HIGH)  36.2 us
    dot_general x8, matrix products, one_slice(): jnp.einsum('cij,kij->ck', act_low, pair_in, preferred_element_type=jnp.fl...  27.9 us
    dot_general x8, matrix products, one_slice(): jnp.einsum('ck,kij->cij', pair_weight, pair_in, preferred_element_type=jn...  21.9 us
    dot_general x8, matrix products, one_slice(): jnp.dot(pre_grad, one_weight.T, preferred_element_type=jnp.float32)  13.5 us
    dynamic_update_slice x8, other arithmetic, local(): lax.scan(one_slice, start, inputs)  11.9 us
    reduce_sum x8, other arithmetic, one_slice(): bias_term = jnp.sum(act_grad, axis=(1, 2))  11.8 us
  transfers between devices with their start and end apart: 3, of which 2 were waited for; matrix products, arithmetic and copies ran while one was open for 48% of the time, Pallas kernels for 0%

commit v1 on v0

--- a/solution.py
+++ b/solution.py
@@ -102,7 +102,9 @@
     hidden_grad = (partial_grad + mean_back[:, None, :] / total_count).astype(jnp.bfloat16)
     mean_term = jnp.dot(mean_rows.astype(jnp.float32).T, column_parts, precision=HIGH)
     grads = (totals[0], totals[1], totals[2], totals[3], mean_term)
-    grads = lax.psum((grads[0], grads[1], grads[2], grads[3], grads[4]), ("slices", "ering"))
+    grads = lax.psum(
+        lax.psum((grads[0], grads[1], grads[2], grads[3], grads[4]), "ering"), "slices"
+    )
     drift = jnp.einsum(
         "cd,sid->csi", drift_weight.astype(jnp.float32), updated.astype(jnp.float32), precision=HIGH
     )

time: 352 us -> 310 us (0.88)
  blocking collectives: 61.6 us -> 36.1 us
  waiting for transfers between devices: 99.3 us -> 80.5 us
    psum x1, blocking collectives: 57.3 us -> 30.6 us  [local(): lax.psum(lax.psum((grads[0], grads[1], grads[2], grads[3], grads[4]), 'er...]
    psum x1 -> x2, waiting for transfers between devices: 90.4 us -> 71.5 us  [the longest x1 71.5 us: local(): lax.psum(lax.psum((grads[0], grads[1], grads[2], grads[3], grads[4]), 'er...]
  transfers between devices with their start and end apart: 3 -> 4, of which waited for: 2 -> 2; matrix products, arithmetic and copies ran while one was open for 48% -> 56% of each run, Pallas kernels for 0% -> 0%
where the time goes in v1:
time: 310 us; the launch traced here: 305 us
  matrix products  132 us (43%)
  waiting for transfers between devices  80.5 us (26%)
  blocking collectives  36.1 us (12%)
  other arithmetic  35.4 us (11%)
  between operations  13.9 us (4%)
  local copies, waits for them, and re-layouts  4.24 us (1%)
    psum x1, waiting for transfers between devices, local(): lax.psum(lax.psum((grads[0], grads[1], grads[2], grads[3], grads[4]), 'er...  71.5 us
    dot_general x8, matrix products, one_slice(): jnp.einsum('ck,kij->cij', embed_weight, features, precision=HIGH)  36.2 us
    psum x1, blocking collectives, local(): lax.psum(lax.psum((grads[0], grads[1], grads[2], grads[3], grads[4]), 'er...  30.6 us
    dot_general x8, matrix products, one_slice(): jnp.einsum('cij,kij->ck', act_low, pair_in, preferred_element_type=jnp.fl...  28 us
    dot_general x8, matrix products, one_slice(): jnp.einsum('ck,kij->cij', pair_weight, pair_in, preferred_element_type=jn...  22 us
    dot_general x8, matrix products, one_slice(): jnp.dot(pre_grad, one_weight.T, preferred_element_type=jnp.float32)  13.6 us
    dynamic_update_slice x8, other arithmetic, local(): lax.scan(one_slice, start, inputs)  11.9 us
    reduce_sum x8, other arithmetic, one_slice(): bias_term = jnp.sum(act_grad, axis=(1, 2))  11.8 us
  transfers between devices with their start and end apart: 4, of which 2 were waited for; matrix products, arithmetic and copies ran while one was open for 56% of the time, Pallas kernels for 0%

profile of v1, /device:TPU:1, one launch (start us, length us, event | category | flops | bytes accessed | tf_op | source)
XLA Modules:
  0.0 305.2 jit_solution(2375710485199730243)
XLA Ops:
  12.8 8.3 %all-gather.2.cloned.1.call-done = bf16[8,256,256]{2,1,0:T(8,128)(2,1)} async-done(((bf16[8,128,256]{2,1,0:T(8,128)(2,1)}), bf16[8,256,256]{2,1,0:T(8,128)(2,1)}) %all-gather.2.cloned.1.call-update) | async-done | bytes 1048592 | tf_op jit(solution)/shard_map/all_gather | solution.py:36
  22.5 160.5 %while.23 = (s32[]{:T(128)}, f32[32,32]{1,0:T(8,128)S(1)}, f32[32]{0:T(128)S(1)}, f32[256,256]{1,0:T(8,128)S(1)}, f32[32,256]{1,0:T(8,128)S(1)}, /*index=5*/bf16...) while((s32[]{:T(128)}, f32[32,32]{1,0:T(8,128)S(1)}, ...), condition=%wide.region_6.7_spmd.clone, body=%wide.region_1.6_spmd.clone.sunk | while | flops 259163936 | bytes 40384416 | solution.py:99
  24.3 4.5 %tanh_convert_fusion.2 = bf16[128,256,32]{1,2,0:T(8,128)(2,1)S(1)} fusion(f32[32]{0:T(128)} %get-tuple-element.457, f32[1,128,256]{2,0,1:T(1,128)S(1)} %copy.37, f32[3,128,256]{2,0,1:T(4,128)S(1)} %get-tuple-element.391, f32[32,4]{0,1:T(4,128)} %get-tuple-element.456), kind=kOutput, calls=%fused_computation.6.clone.1 | convolution fusion | flops 52559872 | bytes 2622080 | tf_op jit(solution)/shard_map/while/body/eval_jaxpr/ck,kij->cij/dot_general | solution.py:45
  33.3 3.5 %fusion.115 = f32[32,32]{1,0:T(8,128)S(1)} fusion(bf16[128,256,32]{1,2,0:T(8,128)(2,1)S(1)} %tanh_convert_fusion.2, f32[128,256,32]{1,2,0:T(8,128)} %get-tuple-element.392, f32[32,128]{0,1:T(8,128)S(1)} %copy.38, f32[32]{0:T(128)S(1)} %copy-done.7, f32[32,32]{1,0:T(8,128)S(1)} %get-tuple-element.421, pred[]{:T(512)S(6)} %compare.3), kind=kOutput, calls=%fused_computation.27.clone.1 | convolution fusion | flops 72353792 | bytes 6316161 | tf_op jit(solution)/shard_map/while/body/eval_jaxpr/cij,kij->ck/dot_general | solution.py:71
  44.3 4.5 %tanh_convert_fusion.2 = bf16[128,256,32]{1,2,0:T(8,128)(2,1)S(1)} fusion(f32[32]{0:T(128)} %get-tuple-element.457, f32[1,128,256]{2,0,1:T(1,128)S(1)} %copy.37, f32[3,128,256]{2,0,1:T(4,128)S(1)} %get-tuple-element.391, f32[32,4]{0,1:T(4,128)} %get-tuple-element.456), kind=kOutput, calls=%fused_computation.6.clone.1 | convolution fusion | flops 52559872 | bytes 2622080 | tf_op jit(solution)/shard_map/while/body/eval_jaxpr/ck,kij->cij/dot_general | solution.py:45
  48.9 2.8 fusion.111
  53.3 3.5 %fusion.115 = f32[32,32]{1,0:T(8,128)S(1)} fusion(bf16[128,256,32]{1,2,0:T(8,128)(2,1)S(1)} %tanh_convert_fusion.2, f32[128,256,32]{1,2,0:T(8,128)} %get-tuple-element.392, f32[32,128]{0,1:T(8,128)S(1)} %copy.38, f32[32]{0:T(128)S(1)} %copy-done.7, f32[32,32]{1,0:T(8,128)S(1)} %get-tuple-element.421, pred[]{:T(512)S(6)} %compare.3), kind=kOutput, calls=%fused_computation.27.clone.1 | convolution fusion | flops 72353792 | bytes 6316161 | tf_op jit(solution)/shard_map/while/body/eval_jaxpr/cij,kij->ck/dot_general | solution.py:71
  64.4 4.5 %tanh_convert_fusion.2 = bf16[128,256,32]{1,2,0:T(8,128)(2,1)S(1)} fusion(f32[32]{0:T(128)} %get-tuple-element.457, f32[1,128,256]{2,0,1:T(1,128)S(1)} %copy.37, f32[3,128,256]{2,0,1:T(4,128)S(1)} %get-tuple-element.391, f32[32,4]{0,1:T(4,128)} %get-tuple-element.456), kind=kOutput, calls=%fused_computation.6.clone.1 | convolution fusion | flops 52559872 | bytes 2622080 | tf_op jit(solution)/shard_map/while/body/eval_jaxpr/ck,kij->cij/dot_general | solution.py:45
  68.9 2.8 fusion.111
  73.4 3.5 %fusion.115 = f32[32,32]{1,0:T(8,128)S(1)} fusion(bf16[128,256,32]{1,2,0:T(8,128)(2,1)S(1)} %tanh_convert_fusion.2, f32[128,256,32]{1,2,0:T(8,128)} %get-tuple-element.392, f32[32,128]{0,1:T(8,128)S(1)} %copy.38, f32[32]{0:T(128)S(1)} %copy-done.7, f32[32,32]{1,0:T(8,128)S(1)} %get-tuple-element.421, pred[]{:T(512)S(6)} %compare.3), kind=kOutput, calls=%fused_computation.27.clone.1 | convolution fusion | flops 72353792 | bytes 6316161 | tf_op jit(solution)/shard_map/while/body/eval_jaxpr/cij,kij->ck/dot_general | solution.py:71
  84.4 4.5 %tanh_convert_fusion.2 = bf16[128,256,32]{1,2,0:T(8,128)(2,1)S(1)} fusion(f32[32]{0:T(128)} %get-tuple-element.457, f32[1,128,256]{2,0,1:T(1,128)S(1)} %copy.37, f32[3,128,256]{2,0,1:T(4,128)S(1)} %get-tuple-element.391, f32[32,4]{0,1:T(4,128)} %get-tuple-element.456), kind=kOutput, calls=%fused_computation.6.clone.1 | convolution fusion | flops 52559872 | bytes 2622080 | tf_op jit(solution)/shard_map/while/body/eval_jaxpr/ck,kij->cij/dot_general | solution.py:45
  89.0 2.8 fusion.111
  93.4 3.5 %fusion.115 = f32[32,32]{1,0:T(8,128)S(1)} fusion(bf16[128,256,32]{1,2,0:T(8,128)(2,1)S(1)} %tanh_convert_fusion.2, f32[128,256,32]{1,2,0:T(8,128)} %get-tuple-element.392, f32[32,128]{0,1:T(8,128)S(1)} %copy.38, f32[32]{0:T(128)S(1)} %copy-done.7, f32[32,32]{1,0:T(8,128)S(1)} %get-tuple-element.421, pred[]{:T(512)S(6)} %compare.3), kind=kOutput, calls=%fused_computation.27.clone.1 | convolution fusion | flops 72353792 | bytes 6316161 | tf_op jit(solution)/shard_map/while/body/eval_jaxpr/cij,kij->ck/dot_general | solution.py:71
  104.5 4.5 %tanh_convert_fusion.2 = bf16[128,256,32]{1,2,0:T(8,128)(2,1)S(1)} fusion(f32[32]{0:T(128)} %get-tuple-element.457, f32[1,128,256]{2,0,1:T(1,128)S(1)} %copy.37, f32[3,128,256]{2,0,1:T(4,128)S(1)} %get-tuple-element.391, f32[32,4]{0,1:T(4,128)} %get-tuple-element.456), kind=kOutput, calls=%fused_computation.6.clone.1 | convolution fusion | flops 52559872 | bytes 2622080 | tf_op jit(solution)/shard_map/while/body/eval_jaxpr/ck,kij->cij/dot_general | solution.py:45
  113.5 3.5 %fusion.115 = f32[32,32]{1,0:T(8,128)S(1)} fusion(bf16[128,256,32]{1,2,0:T(8,128)(2,1)S(1)} %tanh_convert_fusion.2, f32[128,256,32]{1,2,0:T(8,128)} %get-tuple-element.392, f32[32,128]{0,1:T(8,128)S(1)} %copy.38, f32[32]{0:T(128)S(1)} %copy-done.7, f32[32,32]{1,0:T(8,128)S(1)} %get-tuple-element.421, pred[]{:T(512)S(6)} %compare.3), kind=kOutput, calls=%fused_computation.27.clone.1 | convolution fusion | flops 72353792 | bytes 6316161 | tf_op jit(solution)/shard_map/while/body/eval_jaxpr/cij,kij->ck/dot_general | solution.py:71
  124.5 4.5 %tanh_convert_fusion.2 = bf16[128,256,32]{1,2,0:T(8,128)(2,1)S(1)} fusion(f32[32]{0:T(128)} %get-tuple-element.457, f32[1,128,256]{2,0,1:T(1,128)S(1)} %copy.37, f32[3,128,256]{2,0,1:T(4,128)S(1)} %get-tuple-element.391, f32[32,4]{0,1:T(4,128)} %get-tuple-element.456), kind=kOutput, calls=%fused_computation.6.clone.1 | convolution fusion | flops 52559872 | bytes 2622080 | tf_op jit(solution)/shard_map/while/body/eval_jaxpr/ck,kij->cij/dot_general | solution.py:45
  133.5 3.5 %fusion.115 = f32[32,32]{1,0:T(8,128)S(1)} fusion(bf16[128,256,32]{1,2,0:T(8,128)(2,1)S(1)} %tanh_convert_fusion.2, f32[128,256,32]{1,2,0:T(8,128)} %get-tuple-element.392, f32[32,128]{0,1:T(8,128)S(1)} %copy.38, f32[32]{0:T(128)S(1)} %copy-done.7, f32[32,32]{1,0:T(8,128)S(1)} %get-tuple-element.421, pred[]{:T(512)S(6)} %compare.3), kind=kOutput, calls=%fused_computation.27.clone.1 | convolution fusion | flops 72353792 | bytes 6316161 | tf_op jit(solution)/shard_map/while/body/eval_jaxpr/cij,kij->ck/dot_general | solution.py:71
  144.6 4.5 %tanh_convert_fusion.2 = bf16[128,256,32]{1,2,0:T(8,128)(2,1)S(1)} fusion(f32[32]{0:T(128)} %get-tuple-element.457, f32[1,128,256]{2,0,1:T(1,128)S(1)} %copy.37, f32[3,128,256]{2,0,1:T(4,128)S(1)} %get-tuple-element.391, f32[32,4]{0,1:T(4,128)} %get-tuple-element.456), kind=kOutput, calls=%fused_computation.6.clone.1 | convolution fusion | flops 52559872 | bytes 2622080 | tf_op jit(solution)/shard_map/while/body/eval_jaxpr/ck,kij->cij/dot_general | solution.py:45
  153.6 3.5 %fusion.115 = f32[32,32]{1,0:T(8,128)S(1)} fusion(bf16[128,256,32]{1,2,0:T(8,128)(2,1)S(1)} %tanh_convert_fusion.2, f32[128,256,32]{1,2,0:T(8,128)} %get-tuple-element.392, f32[32,128]{0,1:T(8,128)S(1)} %copy.38, f32[32]{0:T(128)S(1)} %copy-done.7, f32[32,32]{1,0:T(8,128)S(1)} %get-tuple-element.421, pred[]{:T(512)S(6)} %compare.3), kind=kOutput, calls=%fused_computation.27.clone.1 | convolution fusion | flops 72353792 | bytes 6316161 | tf_op jit(solution)/shard_map/while/body/eval_jaxpr/cij,kij->ck/dot_general | solution.py:71
  164.6 4.5 %tanh_convert_fusion.2 = bf16[128,256,32]{1,2,0:T(8,128)(2,1)S(1)} fusion(f32[32]{0:T(128)} %get-tuple-element.457, f32[1,128,256]{2,0,1:T(1,128)S(1)} %copy.37, f32[3,128,256]{2,0,1:T(4,128)S(1)} %get-tuple-element.391, f32[32,4]{0,1:T(4,128)} %get-tuple-element.456), kind=kOutput, calls=%fused_computation.6.clone.1 | convolution fusion | flops 52559872 | bytes 2622080 | tf_op jit(solution)/shard_map/while/body/eval_jaxpr/ck,kij->cij/dot_general | solution.py:45
  173.7 3.5 %fusion.115 = f32[32,32]{1,0:T(8,128)S(1)} fusion(bf16[128,256,32]{1,2,0:T(8,128)(2,1)S(1)} %tanh_convert_fusion.2, f32[128,256,32]{1,2,0:T(8,128)} %get-tuple-element.392, f32[32,128]{0,1:T(8,128)S(1)} %copy.38, f32[32]{0:T(128)S(1)} %copy-done.7, f32[32,32]{1,0:T(8,128)S(1)} %get-tuple-element.421, pred[]{:T(512)S(6)} %compare.3), kind=kOutput, calls=%fused_computation.27.clone.1 | convolution fusion | flops 72353792 | bytes 6316161 | tf_op jit(solution)/shard_map/while/body/eval_jaxpr/cij,kij->ck/dot_general | solution.py:71
  186.0 3.7 %all-reduce.2 = (f32[8,256]{1,0:T(8,128)S(1)}, f32[32,32]{1,0:T(8,128)S(1)}, f32[32]{0:T(128)S(1)}, f32[32,256]{1,0:T(8,128)S(1)}) all-reduce(f32[8,256]{1,0:T(8,128)S(1)} %get-tuple-element.123, f32[32,32]{1,0:T(8,128)S(1)} %get-tuple-element.124, ...), channel_id=1, replica_groups=mesh['groups'=2,'slices'=8,'ering'=2] {'ering'}, use_global_device_ids=true, to_apply=%region_7.8 | all-reduce | flops 11296 | bytes 90368 | tf_op jit(solution)/shard_map/psum | solution.py:100
  189.8 30.6 %all-reduce = (f32[32,32]{1,0:T(8,128)S(1)}, f32[32]{0:T(128)S(1)}, f32[32,256]{1,0:T(8,128)S(1)}) all-reduce(f32[32,32]{1,0:T(8,128)S(1)} %get-tuple-element.242, f32[32]{0:T(128)S(1)} %get-tuple-element.243, f32[32,256]{1,0:T(8,128)S(1)} %get-tuple-element.244), channel_id=1, replica_groups=mesh['groups'=2,'slices'=8,'ering'=2] {'slices'}, use_global_device_ids=true, to_apply=%region_10.11 | all-reduce | flops 9248 | bytes 73984 | tf_op jit(solution)/shard_map/psum | solution.py:105
  225.4 71.5 %all-reduce.7.cloned.1.call-done = (f32[256,256]{1,0:T(8,128)}, f32[256,256]{1,0:T(8,128)}) async-done(((f32[256,256]{1,0:T(8,128)}, f32[256,256]{1,0:T(8,128)}), (f32[256,256]{1,0:T(8,128)}, f32[256,256]{1,0:T(8,128)})) %all-reduce.7.cloned.1.call-update) | async-done | bytes 524304 | tf_op jit(solution)/shard_map/psum | solution.py:105
  (276 shorter events, 103.6 us)
Async XLA Ops:
  7.2 176.9 %copy-start = (bf16[3,256]{1,0:T(4,128)(2,1)S(1)}, bf16[3,256]{1,0:T(4,128)(2,1)}, u32[]{:S(2)}) copy-start(bf16[3,256]{1,0:T(4,128)(2,1)} %param.25) | copy-start | bytes 4612
  7.2 13.9 %all-gather.2.cloned.1.call-start = ((), (), s32[]{:S(2)}) async-start(), calls=%async_computation | async-start | bytes 1572864 | tf_op jit(solution)/shard_map/all_gather | solution.py:36
  7.9 213.6 %all-reduce.9.cloned.1.call-start = ((), (), s32[]{:S(2)}) async-start(), calls=%async_computation.2 | async-start | bytes 1048576 | tf_op jit(solution)/shard_map/psum | solution.py:106
  8.7 175.4 %collective-permute-start = (f32[3,1,128]{2,0,1:T(4,128)S(1)}, f32[3,1,128]{2,0,1:T(4,128)S(1)}, u32[]{:S(2)}, u32[]{:S(2)}) collective-permute-start(f32[3,1,128]{2,0,1:T(4,128)S(1)} %slice.9), channel_id=1, source_target_pairs={{2,0},{4,2},{6,4},{8,6},{10,8},{12,10},{14,12},{3,1},{5,3},{7,5},{... | collective-permute-start | bytes 4616 | tf_op jit(solution)/shard_map/ppermute | solution.py:14
  22.5 161.6 %copy-start.6 = (f32[3,8,128]{2,1,0:T(8,128)S(1)}, f32[3,8,128]{2,1,0:T(8,128)}, u32[]{:S(2)}) copy-start(f32[3,8,128]{2,1,0:T(8,128)} %param.14) | copy-start | bytes 36868
  24.2 7.5 %copy-start.2 = (bf16[256,256]{1,0:T(8,128)(2,1)S(1)}, bf16[256,256]{1,0:T(8,128)(2,1)}, u32[]{:S(2)}) copy-start(bf16[256,256]{1,0:T(8,128)(2,1)} %get-tuple-element.453) | copy-start | bytes 393220 | tf_op jit(solution)/shard_map/while
  24.2 7.5 %copy-start.8 = (f32[256]{0:T(256)S(1)}, f32[256]{0:T(256)}, u32[]{:S(2)}) copy-start(f32[256]{0:T(256)} %get-tuple-element.463) | copy-start | bytes 3076 | tf_op jit(solution)/shard_map/while
  44.3 7.5 %copy-start.2 = (bf16[256,256]{1,0:T(8,128)(2,1)S(1)}, bf16[256,256]{1,0:T(8,128)(2,1)}, u32[]{:S(2)}) copy-start(bf16[256,256]{1,0:T(8,128)(2,1)} %get-tuple-element.453) | copy-start | bytes 393220 | tf_op jit(solution)/shard_map/while
  44.3 7.5 %copy-start.8 = (f32[256]{0:T(256)S(1)}, f32[256]{0:T(256)}, u32[]{:S(2)}) copy-start(f32[256]{0:T(256)} %get-tuple-element.463) | copy-start | bytes 3076 | tf_op jit(solution)/shard_map/while
  64.3 7.5 %copy-start.2 = (bf16[256,256]{1,0:T(8,128)(2,1)S(1)}, bf16[256,256]{1,0:T(8,128)(2,1)}, u32[]{:S(2)}) copy-start(bf16[256,256]{1,0:T(8,128)(2,1)} %get-tuple-element.453) | copy-start | bytes 393220 | tf_op jit(solution)/shard_map/while
  64.3 7.5 %copy-start.8 = (f32[256]{0:T(256)S(1)}, f32[256]{0:T(256)}, u32[]{:S(2)}) copy-start(f32[256]{0:T(256)} %get-tuple-element.463) | copy-start | bytes 3076 | tf_op jit(solution)/shard_map/while
  84.4 7.5 %copy-start.2 = (bf16[256,256]{1,0:T(8,128)(2,1)S(1)}, bf16[256,256]{1,0:T(8,128)(2,1)}, u32[]{:S(2)}) copy-start(bf16[256,256]{1,0:T(8,128)(2,1)} %get-tuple-element.453) | copy-start | bytes 393220 | tf_op jit(solution)/shard_map/while
  84.4 7.5 %copy-start.8 = (f32[256]{0:T(256)S(1)}, f32[256]{0:T(256)}, u32[]{:S(2)}) copy-start(f32[256]{0:T(256)} %get-tuple-element.463) | copy-start | bytes 3076 | tf_op jit(solution)/shard_map/while
  104.4 7.5 %copy-start.2 = (bf16[256,256]{1,0:T(8,128)(2,1)S(1)}, bf16[256,256]{1,0:T(8,128)(2,1)}, u32[]{:S(2)}) copy-start(bf16[256,256]{1,0:T(8,128)(2,1)} %get-tuple-element.453) | copy-start | bytes 393220 | tf_op jit(solution)/shard_map/while
  104.5 7.5 %copy-start.8 = (f32[256]{0:T(256)S(1)}, f32[256]{0:T(256)}, u32[]{:S(2)}) copy-start(f32[256]{0:T(256)} %get-tuple-element.463) | copy-start | bytes 3076 | tf_op jit(solution)/shard_map/while
  124.5 7.5 %copy-start.2 = (bf16[256,256]{1,0:T(8,128)(2,1)S(1)}, bf16[256,256]{1,0:T(8,128)(2,1)}, u32[]{:S(2)}) copy-start(bf16[256,256]{1,0:T(8,128)(2,1)} %get-tuple-element.453) | copy-start | bytes 393220 | tf_op jit(solution)/shard_map/while
  124.5 7.5 %copy-start.8 = (f32[256]{0:T(256)S(1)}, f32[256]{0:T(256)}, u32[]{:S(2)}) copy-start(f32[256]{0:T(256)} %get-tuple-element.463) | copy-start | bytes 3076 | tf_op jit(solution)/shard_map/while
  144.6 7.3 %copy-start.4 = (bf16[32,256]{1,0:T(8,128)(2,1)S(1)}, bf16[32,256]{1,0:T(8,128)(2,1)}, u32[]{:S(2)}) copy-start(bf16[32,256]{1,0:T(8,128)(2,1)} %get-tuple-element.460) | copy-start | bytes 49156 | tf_op jit(solution)/shard_map/while
  144.6 7.5 %copy-start.2 = (bf16[256,256]{1,0:T(8,128)(2,1)S(1)}, bf16[256,256]{1,0:T(8,128)(2,1)}, u32[]{:S(2)}) copy-start(bf16[256,256]{1,0:T(8,128)(2,1)} %get-tuple-element.453) | copy-start | bytes 393220 | tf_op jit(solution)/shard_map/while
  144.6 7.5 %copy-start.8 = (f32[256]{0:T(256)S(1)}, f32[256]{0:T(256)}, u32[]{:S(2)}) copy-start(f32[256]{0:T(256)} %get-tuple-element.463) | copy-start | bytes 3076 | tf_op jit(solution)/shard_map/while
  164.6 7.3 %copy-start.4 = (bf16[32,256]{1,0:T(8,128)(2,1)S(1)}, bf16[32,256]{1,0:T(8,128)(2,1)}, u32[]{:S(2)}) copy-start(bf16[32,256]{1,0:T(8,128)(2,1)} %get-tuple-element.460) | copy-start | bytes 49156 | tf_op jit(solution)/shard_map/while
  164.6 7.5 %copy-start.2 = (bf16[256,256]{1,0:T(8,128)(2,1)S(1)}, bf16[256,256]{1,0:T(8,128)(2,1)}, u32[]{:S(2)}) copy-start(bf16[256,256]{1,0:T(8,128)(2,1)} %get-tuple-element.453) | copy-start | bytes 393220 | tf_op jit(solution)/shard_map/while
  164.6 7.5 %copy-start.8 = (f32[256]{0:T(256)S(1)}, f32[256]{0:T(256)}, u32[]{:S(2)}) copy-start(f32[256]{0:T(256)} %get-tuple-element.463) | copy-start | bytes 3076 | tf_op jit(solution)/shard_map/while
  184.0 112.8 %all-reduce.7.cloned.1.call-start = ((), (), s32[]{:S(2)}) async-start(), calls=%async_computation.1 | async-start | bytes 1048576 | tf_op jit(solution)/shard_map/psum | solution.py:105
  (31 other events, 173.9 us)
Sparse Core Ops, SparseCore 0:
  9.6 11.4 all-gather.1
  184.1 19.9 all-reduce.8
  221.7 75.0 all-reduce.6
